TPU v7x, 256 devices: a whole 4x4x8 slice. The times are simulated.
256 devices in a mesh: diag: 32 (over y, z_lo, core), tri: 8 (over z_hi, x).
Axes of the slice: x: 4, y: 4, z: 8 (z_hi: 2, z_lo: 4; z = z_hi * 4 + z_lo), core: 2. Of those that a mesh axis runs over, the one named last changes fastest.
Arguments:
- trial_sets: bfloat16 [2, 12, 131072], P(None, None, 'diag'), may hold values from -6 to 6
- tile_values: bfloat16 [32, 8, 192, 128, 128], P('diag', 'tri'), may hold values from -0.0546875 to 0.0546875
- tile_pattern: int32 [32, 8, 2, 192], P('diag', 'tri'), may hold values from 0 to 31, as said below
- tile_count: int32 [32, 8], P('diag', 'tri'), may hold values from 48 to 192, as said below
Outputs:
- images: float32 [2, 12, 131072], P(None, None, ('diag', 'tri'))
Inputs may be any that keep to these rules, and one draw needn't show every extreme that they name: `tile_pattern`: within each stored block the live and padding slots name distinct tiles. `tile_count`: some stored block has all 192 slots live.
All inputs are finite; a program needn't handle non-finite values.
Results may differ from a plain program's by a relative error of at most 0.0003.
Values may be sent and summed in bfloat16 or wider, within the bound.
A program may use at most 64 MiB of HBM per device.

v0:
```python
import jax
import jax.numpy as jnp
from jax import lax
from jax.sharding import PartitionSpec as P


def passed_along(x, axis, by):
    count = lax.axis_size(axis)
    return lax.ppermute(x, axis, [(i, (i + by) % count) for i in range(count)])


def local(trial_sets, tile_values, tile_pattern, tile_count):
    set_count, vec_count, row_total = trial_sets.shape
    columns = set_count * vec_count
    tile_data = tile_values[0, 0]
    tile_total = tile_data.shape[0]
    tile_size = tile_data.shape[1]
    blocks = row_total // tile_size
    tile_rows = tile_pattern[0, 0, 0]
    tile_cols = tile_pattern[0, 0, 1]
    live_mask = (jnp.arange(tile_total) < tile_count[0, 0]).astype(jnp.float32)
    tri_index = lax.axis_index("tri")
    tri_total = lax.axis_size("tri")
    bit_count = tri_total.bit_length() - 1
    own_block = trial_sets.reshape(columns, blocks, tile_size)
    held_block = own_block
    for bit_index in range(bit_count):
        moved = passed_along(held_block, "diag", 1 << bit_index)
        bit_set = tri_index >> bit_index & 1 == 1
        held_block = jnp.where(bit_set, moved, held_block)
    tile_axis = jnp.arange(blocks)
    picked_cols = jnp.take(held_block, tile_cols, axis=1)
    row_terms = jnp.einsum(
        "nab,vnb->vna", tile_data, picked_cols, preferred_element_type=jnp.float32
    )
    row_hot = (tile_rows[:, None] == tile_axis[None, :]).astype(jnp.float32) * live_mask[:, None]
    row_part = jnp.einsum("vna,nr->vra", row_terms, row_hot, precision=lax.Precision.HIGHEST)
    picked_rows = jnp.take(own_block, tile_rows, axis=1)
    col_terms = jnp.einsum(
        "nab,vna->vnb", tile_data, picked_rows, preferred_element_type=jnp.float32
    )
    col_hot = (tile_cols[:, None] == tile_axis[None, :]).astype(jnp.float32) * live_mask[:, None]
    col_part = jnp.einsum("vnb,nr->vrb", col_terms, col_hot, precision=lax.Precision.HIGHEST)
    carried = col_part
    for bit_index in range(bit_count):
        moved = passed_along(carried, "diag", -(1 << bit_index))
        bit_set = tri_index >> bit_index & 1 == 1
        carried = jnp.where(bit_set, moved, carried)
    combined = row_part + carried
    combined = combined.reshape(columns, row_total)
    images = lax.psum_scatter(combined, "tri", scatter_dimension=1, tiled=True)
    return images.reshape(set_count, vec_count, row_total // tri_total)


def solution(mesh):
    return jax.shard_map(
        local,
        mesh=mesh,
        in_specs=(
            P(None, None, "diag"),
            P("diag", "tri", None, None, None),
            P("diag", "tri", None, None),
            P("diag", "tri"),
        ),
        out_specs=P(None, None, ("diag", "tri")),
        check_vma=False,
    )
```

profile of v0, /device:TPU:1, one launch (start us, length us, event | category | flops | bytes accessed | tf_op | source)
XLA Modules:
  0.0 167.1 jit_solution(10166838583431014875)
XLA Ops:
  6.5 0.0 reduce-scatter.2.cloned.1.call-start
  6.5 1.0 copy.6
  7.6 0.2 reshape.21
  7.7 3.1 %collective-permute-start = (bf16[24,32,128]{2,1,0:T(8,128)(2,1)S(1)}, bf16[24,32,128]{2,1,0:T(8,128)(2,1)S(1)}, u32[]{:S(2)}, u32[]{:S(2)}) collective-permute-start(bf16[24,32,128]{2,1,0:T(8,128)(2,1)S(1)} %reshape.21), channel_id=1, source_target_pairs={{0,8},{8,16},{16,24},{24,32},{32,40},{40,48},{48,56},{56,64},{64,7... | collective-permute-start | bytes 589832 | tf_op jit(solution)/shard_map/ppermute | solution.py:9
  10.8 0.1 copy.8
  10.9 0.8 fusion.38
  12.4 0.9 gather_fusion.1
  13.3 3.9 %fusion = f32[192,24,128]{2,1,0:T(8,128)S(1)} fusion(bf16[1,1,192,128,128]{4,3,2,1,0:T(8,128)(2,1)} %param.7, bf16[192,24,128]{2,1,0:T(8,128)(2,1)S(1)} %gather_fusion.1, pred[192]{0:T(512)(128)(4,1)S(1)} %compare_and_fusion), kind=kOutput, calls=%fused_computation.2 | convolution fusion | flops 151584768 | bytes 9830592 | tf_op jit(solution)/shard_map/nab,vna->vnb/dot_general | solution.py:39
  17.2 1.8 %fusion.13 = f32[24,32,128]{2,1,0:T(8,128)S(1)} fusion(f32[192,24,128]{2,1,0:T(8,128)S(1)} %fusion, s32[192]{0:T(256)S(1)} %bitcast.44, f32[192]{0:T(256)S(1)} %compare_convert_fusion), kind=kOutput, calls=%fused_computation.13 | convolution fusion | flops 226504704 | bytes 2754048 | tf_op jit(solution)/shard_map/vnb,nr->vrb/dot_general | solution.py:43
  19.0 0.3 collective-permute-start.3
  19.3 0.0 collective-permute-done
  19.3 1.5 collective-permute-start.1
  20.8 7.5 %collective-permute-done.1 = bf16[24,32,128]{2,1,0:T(8,128)(2,1)S(1)} collective-permute-done((bf16[24,32,128]{2,1,0:T(8,128)(2,1)S(1)}, bf16[24,32,128]{2,1,0:T(8,128)(2,1)S(1)}, u32[]{:S(2)}, u32[]{:S(2)}) %collective-permute-start.1) | collective-permute-done | bytes 196640 | tf_op jit(solution)/shard_map/ppermute | solution.py:9
  28.4 0.1 collective-permute-start.2
  28.6 0.0 collective-permute-done.3
  28.6 0.1 broadcast_select_fusion
  28.6 8.0 %collective-permute-start.4 = (f32[24,32,128]{2,1,0:T(8,128)S(1)}, f32[24,32,128]{2,1,0:T(8,128)S(1)}, u32[]{:S(2)}, u32[]{:S(2)}) collective-permute-start(f32[24,32,128]{2,1,0:T(8,128)S(1)} %broadcast_select_fusion), channel_id=1, source_target_pairs={{0,240},{8,248},{16,0},{24,8},{32,16},{40,24},{48,32},{56,40},{64,... | collective-permute-start | bytes 1179656 | tf_op jit(solution)/shard_map/ppermute | solution.py:9
  36.6 1.7 %collective-permute-done.2 = bf16[24,32,128]{2,1,0:T(8,128)(2,1)S(1)} collective-permute-done((bf16[24,32,128]{2,1,0:T(8,128)(2,1)S(1)}, bf16[24,32,128]{2,1,0:T(8,128)(2,1)S(1)}, u32[]{:S(2)}, u32[]{:S(2)}) %collective-permute-start.2) | collective-permute-done | bytes 196640 | tf_op jit(solution)/shard_map/ppermute | solution.py:9
  38.4 0.1 copy.7
  38.5 0.9 gather_fusion
  39.4 5.3 %collective-permute-done.4 = f32[24,32,128]{2,1,0:T(8,128)S(1)} collective-permute-done((f32[24,32,128]{2,1,0:T(8,128)S(1)}, f32[24,32,128]{2,1,0:T(8,128)S(1)}, u32[]{:S(2)}, u32[]{:S(2)}) %collective-permute-start.4) | collective-permute-done | bytes 393248 | tf_op jit(solution)/shard_map/ppermute | solution.py:9
  44.7 0.1 broadcast_select_fusion.2
  44.7 0.3 collective-permute-start.5
  45.0 5.6 %fusion.2 = f32[192,24,128]{2,1,0:T(8,128)S(1)} fusion(bf16[1,1,192,128,128]{4,3,2,1,0:T(8,128)(2,1)} %param.7, bf16[192,24,128]{2,1,0:T(8,128)(2,1)S(1)} %gather_fusion, pred[192]{0:T(512)(128)(4,1)S(1)} %compare_and_fusion.1), kind=kOutput, calls=%fused_computation.4 | convolution fusion | flops 151584768 | bytes 9830592 | tf_op jit(solution)/shard_map/nab,vnb->vna/dot_general | solution.py:33
  50.6 1.8 %fusion.10 = f32[24,32,128]{2,1,0:T(8,128)S(1)} fusion(f32[192,24,128]{2,1,0:T(8,128)S(1)} %fusion.2, f32[192]{0:T(256)S(1)} %compare_convert_fusion, s32[192]{0:T(256)S(1)} %bitcast.43), kind=kOutput, calls=%fused_computation.12 | convolution fusion | flops 226504704 | bytes 2754048 | tf_op jit(solution)/shard_map/vna,nr->vra/dot_general | solution.py:37
  52.4 8.9 %collective-permute-done.5 = f32[24,32,128]{2,1,0:T(8,128)S(1)} collective-permute-done((f32[24,32,128]{2,1,0:T(8,128)S(1)}, f32[24,32,128]{2,1,0:T(8,128)S(1)}, u32[]{:S(2)}, u32[]{:S(2)}) %collective-permute-start.5) | collective-permute-done | bytes 393248 | tf_op jit(solution)/shard_map/ppermute | solution.py:9
  61.2 0.1 select_add_fusion
  61.3 1.0 copy.26
  62.3 0.0 reduce-scatter.2.cloned.1.call-update
  62.3 96.5 %reduce-scatter.2.cloned.1.call-done = f32[24,512]{1,0:T(8,128)} async-done(((f32[24,4096]{1,0:T(8,128)}), f32[24,512]{1,0:T(8,128)}) %reduce-scatter.2.cloned.1.call-update) | async-done | bytes 49168 | tf_op jit(solution)/shard_map/reduce_scatter | solution.py:51
  158.8 0.8 reshape.23
  159.6 0.7 copy.9
  (10 shorter events, 0.1 us)
Async XLA Ops:
  6.5 152.3 %reduce-scatter.2.cloned.1.call-start = ((), (), s32[]{:S(2)}) async-start(), calls=%async_computation.1 | async-start | bytes 442368 | tf_op jit(solution)/shard_map/reduce_scatter | solution.py:51
  7.7 11.5 %collective-permute-start = (bf16[24,32,128]{2,1,0:T(8,128)(2,1)S(1)}, bf16[24,32,128]{2,1,0:T(8,128)(2,1)S(1)}, u32[]{:S(2)}, u32[]{:S(2)}) collective-permute-start(bf16[24,32,128]{2,1,0:T(8,128)(2,1)S(1)} %reshape.21), channel_id=1, source_target_pairs={{0,8},{8,16},{16,24},{24,32},{32,40},{40,48},{48,56},{56,64},{64,7... | collective-permute-start | bytes 589832 | tf_op jit(solution)/shard_map/ppermute | solution.py:9
  19.0 9.6 %collective-permute-start.3 = (f32[24,32,128]{2,1,0:T(8,128)S(1)}, f32[24,32,128]{2,1,0:T(8,128)S(1)}, u32[]{:S(2)}, u32[]{:S(2)}) collective-permute-start(f32[24,32,128]{2,1,0:T(8,128)S(1)} %fusion.13), channel_id=1, source_target_pairs={{0,248},{8,0},{16,8},{24,16},{32,24},{40,32},{48,40},{56,48},{64,5... | collective-permute-start | bytes 1179656 | tf_op jit(solution)/shard_map/ppermute | solution.py:9
  19.3 9.1 %collective-permute-start.1 = (bf16[24,32,128]{2,1,0:T(8,128)(2,1)S(1)}, bf16[24,32,128]{2,1,0:T(8,128)(2,1)S(1)}, u32[]{:S(2)}, u32[]{:S(2)}) collective-permute-start(bf16[24,32,128]{2,1,0:T(8,128)(2,1)S(1)} %broadcast_select_fusion.1), channel_id=1, source_target_pairs={{0,16},{8,24},{16,32},{24,40},{32,48},{40,56},{48,64},{56,72},{64,... | collective-permute-start | bytes 589832 | tf_op jit(solution)/shard_map/ppermute | solution.py:9
  28.4 10.0 %collective-permute-start.2 = (bf16[24,32,128]{2,1,0:T(8,128)(2,1)S(1)}, bf16[24,32,128]{2,1,0:T(8,128)(2,1)S(1)}, u32[]{:S(2)}, u32[]{:S(2)}) collective-permute-start(bf16[24,32,128]{2,1,0:T(8,128)(2,1)S(1)} %broadcast_select_fusion.3), channel_id=1, source_target_pairs={{0,32},{8,40},{16,48},{24,56},{32,64},{40,72},{48,80},{56,88},{64,... | collective-permute-start | bytes 589832 | tf_op jit(solution)/shard_map/ppermute | solution.py:9
  28.6 16.0 %collective-permute-start.4 = (f32[24,32,128]{2,1,0:T(8,128)S(1)}, f32[24,32,128]{2,1,0:T(8,128)S(1)}, u32[]{:S(2)}, u32[]{:S(2)}) collective-permute-start(f32[24,32,128]{2,1,0:T(8,128)S(1)} %broadcast_select_fusion), channel_id=1, source_target_pairs={{0,240},{8,248},{16,0},{24,8},{32,16},{40,24},{48,32},{56,40},{64,... | collective-permute-start | bytes 1179656 | tf_op jit(solution)/shard_map/ppermute | solution.py:9
  44.7 16.5 %collective-permute-start.5 = (f32[24,32,128]{2,1,0:T(8,128)S(1)}, f32[24,32,128]{2,1,0:T(8,128)S(1)}, u32[]{:S(2)}, u32[]{:S(2)}) collective-permute-start(f32[24,32,128]{2,1,0:T(8,128)S(1)} %broadcast_select_fusion.2), channel_id=1, source_target_pairs={{0,224},{8,232},{16,240},{24,248},{32,0},{40,8},{48,16},{56,24},{6... | collective-permute-start | bytes 1179656 | tf_op jit(solution)/shard_map/ppermute | solution.py:9
Sparse Core Ops, SparseCore 0:
  62.5 96.3 reduce-scatter.1
where the time goes:
time: 168 us; the launch traced here: 167 us
  waiting for transfers between devices  120 us (71%)
  between operations  14.2 us (8%)
  starting transfers between devices  13.3 us (8%)
  matrix products  13 us (8%)
  local copies, waits for them, and re-layouts  6.36 us (4%)
    reduce_scatter x1, waiting for transfers between devices, local(): images = lax.psum_scatter(combined, 'tri', scatter_dimension=1, tiled=True)  96.5 us
    ppermute x6, waiting for transfers between devices, passed_along(): return lax.ppermute(x, axis, [(i, (i + by) % count) for i in range(count)])  23.4 us
    ppermute x6, starting transfers between devices, passed_along(): return lax.ppermute(x, axis, [(i, (i + by) % count) for i in range(count)])  13.3 us
    dot_general x1, matrix products, local(): jnp.einsum('nab,vnb->vna', tile_data, picked_cols, preferred_element_type...  5.58 us
    dot_general x1, matrix products, local(): jnp.einsum('nab,vna->vnb', tile_data, picked_rows, preferred_element_type...  3.92 us
  transfers between devices with their start and end apart: 7, of which 5 were waited for; matrix products, arithmetic and copies ran while one was open for 10% of the time, Pallas kernels for 0%

commit v1 on v0

v1 whole, which is shorter than its diff:
```python
import functools

import jax
import jax.numpy as jnp
from jax import lax
from jax.experimental import pallas as pl
from jax.experimental.pallas import tpu as pltpu
from jax.sharding import PartitionSpec as P

MESH = pl.DeviceIdType.MESH
GROUP = 32


def place(tile):
    return ((tile >> 2) & 3) * 8 + (tile >> 4) * 4 + (tile & 3)


def product_kernel(transposed, pattern, count, x_ref, tiles_ref, out_ref):
    step = pl.program_id(0)

    @pl.when(step == 0)
    def _():
        out_ref[...] = jnp.zeros_like(out_ref)

    live = count[0, 0]
    source, target = (1, 0) if transposed else (0, 1)
    contract = (((1,), (1,)), ((), ())) if transposed else (((1,), (0,)), ((), ()))

    for part in range(GROUP // 8):
        terms = []
        for u in range(8):
            slot = step * GROUP + part * 8 + u
            term = lax.dot_general(
                x_ref[pattern[source, slot]],
                tiles_ref[part * 8 + u],
                contract,
                preferred_element_type=jnp.float32,
            )
            terms.append(jnp.where(slot < live, term, 0.0))
        for u in range(8):
            slot = step * GROUP + part * 8 + u
            where = place(pattern[target, slot])
            out_ref[where] += terms[u]


def product(transposed, pattern, count, x, tiles):
    blocks, columns, size = x.shape
    total = tiles.shape[0]
    return pl.pallas_call(
        functools.partial(product_kernel, transposed),
        out_shape=jax.ShapeDtypeStruct((blocks, columns, size), jnp.float32),
        grid=(total // GROUP,),
        in_specs=[
            pl.BlockSpec(memory_space=pltpu.SMEM),
            pl.BlockSpec(memory_space=pltpu.SMEM),
            pl.BlockSpec((blocks, columns, size), lambda i: (0, 0, 0)),
            pl.BlockSpec((GROUP, size, size), lambda i: (i, 0, 0)),
        ],
        out_specs=pl.BlockSpec((blocks, columns, size), lambda i: (0, 0, 0)),
        cost_estimate=pl.CostEstimate(
            flops=2 * total * columns * size * size,
            bytes_accessed=2 * total * size * size + 6 * blocks * columns * size,
            transcendentals=0,
        ),
        name="row_product" if transposed else "col_product",
    )(pattern, count, x, tiles)


def reduce_kernel(row_ref, col_ref, out_ref, total, got, half, got_half, send, recv, zsem):
    tri = lax.axis_index("tri")
    x, z = tri % 4, tri // 4
    barrier = pltpu.get_barrier_semaphore()
    for d in range(1, 4):
        pl.semaphore_signal(barrier, inc=1, device_id={"tri": z * 4 + (x + d) % 4}, device_id_type=MESH)
    pl.semaphore_signal(barrier, inc=1, device_id={"tri": (1 - z) * 4 + x}, device_id_type=MESH)
    total[...] = row_ref[...] + col_ref[...]
    pl.semaphore_wait(barrier, 4)
    copies = []
    for d in (2, 1, 3):
        peer = (x + d) % 4
        copy = pltpu.make_async_remote_copy(
            src_ref=total.at[pl.ds(peer * 8, 8)],
            dst_ref=got.at[d - 1],
            send_sem=send.at[d - 1],
            recv_sem=recv.at[d - 1],
            device_id={"tri": z * 4 + peer},
            device_id_type=MESH,
        )
        copy.start()
        copies.append(copy)
    for copy in copies:
        copy.wait_recv()
    theirs, mine = (1 - z) * 4, z * 4
    half[0] = total[pl.ds(x * 8 + theirs, 4)] + got[0, pl.ds(theirs, 4)] + got[1, pl.ds(theirs, 4)] + got[2, pl.ds(theirs, 4)]
    half[1] = total[pl.ds(x * 8 + mine, 4)] + got[0, pl.ds(mine, 4)] + got[1, pl.ds(mine, 4)] + got[2, pl.ds(mine, 4)]
    across = pltpu.make_async_remote_copy(
        src_ref=half.at[0],
        dst_ref=got_half,
        send_sem=zsem.at[0],
        recv_sem=zsem.at[1],
        device_id={"tri": (1 - z) * 4 + x},
        device_id_type=MESH,
    )
    across.start()
    for copy in copies:
        copy.wait_send()
    across.wait()
    for j in range(4):
        out_ref[:, j * 128 : (j + 1) * 128] = half[1, j] + got_half[j]


def reduced(row, col):
    blocks, columns, size = row.shape
    return pl.pallas_call(
        reduce_kernel,
        out_shape=jax.ShapeDtypeStruct((columns, blocks * size // 8), jnp.float32),
        in_specs=[pl.BlockSpec(memory_space=pltpu.VMEM)] * 2,
        out_specs=pl.BlockSpec(memory_space=pltpu.VMEM),
        scratch_shapes=[
            pltpu.VMEM((blocks, columns, size), jnp.float32),
            pltpu.VMEM((3, 8, columns, size), jnp.float32),
            pltpu.VMEM((2, 4, columns, size), jnp.float32),
            pltpu.VMEM((4, columns, size), jnp.float32),
            pltpu.SemaphoreType.DMA((3,)),
            pltpu.SemaphoreType.DMA((3,)),
            pltpu.SemaphoreType.DMA((2,)),
        ],
        compiler_params=pltpu.CompilerParams(collective_id=0, has_side_effects=True),
        name="reduce_tri",
    )(row, col)


def local(trial_sets, tile_values, tile_pattern, tile_count):
    sets, vecs, rows = trial_sets.shape
    columns = sets * vecs
    size = tile_values.shape[-1]
    blocks = rows // size
    own = trial_sets.transpose(1, 0, 2).reshape(columns, blocks, size).transpose(1, 0, 2)
    diag, tri = lax.axis_size("diag"), lax.axis_size("tri")
    pairs = [(i * tri + k, (i + k) % diag * tri + k) for i in range(diag) for k in range(tri)]
    held = lax.ppermute(own, ("diag", "tri"), pairs)
    pattern, tiles = tile_pattern[0, 0], tile_values[0, 0]
    col = product(False, pattern, tile_count, own, tiles)
    back = lax.ppermute(col, ("diag", "tri"), [(b, a) for a, b in pairs])
    row = product(True, pattern, tile_count, held, tiles)
    out = reduced(row, back)
    return out.reshape(vecs, sets, rows // tri).transpose(1, 0, 2)


def solution(mesh):
    return jax.shard_map(
        local,
        mesh=mesh,
        in_specs=(
            P(None, None, "diag"),
            P("diag", "tri", None, None, None),
            P("diag", "tri", None, None),
            P("diag", "tri"),
        ),
        out_specs=P(None, None, ("diag", "tri")),
        check_vma=False,
    )
```

time: 168 us -> 71.3 us (0.42)
  waiting for transfers between devices: 120 us -> 0.01 us
  Pallas kernels: 0 us -> 63.1 us
  between operations: 14.2 us -> 0.73 us
  matrix products: 13 us -> 0 us
  starting transfers between devices: 13.3 us -> 2.3 us
    reduce_scatter x1 -> x0, waiting for transfers between devices: 96.5 us -> none  [local(): images = lax.psum_scatter(combined, 'tri', scatter_dimension=1, tiled=True)]
    pallas_call x0 -> x3, Pallas kernels: none -> 63.1 us  [the longest x1 49.3 us: reduced(): pl.pallas_call(reduce_kernel, out_shape=jax.ShapeDtypeStruct((columns, bl...]
    ppermute x6 -> x2, waiting for transfers between devices: 23.4 us -> 0.01 us  [the longest x1 0.01 us: local(): held = lax.ppermute(own, ('diag', 'tri'), pairs)]
    dot_general x4 -> x0, matrix products: 13 us -> none  [the longest x1 5.58 us: local(): jnp.einsum('nab,vnb->vna', tile_data, picked_cols, preferred_element_type...]
    ppermute x6 -> x2, starting transfers between devices: 13.3 us -> 2.3 us  [the longest x1 1.64 us: local(): back = lax.ppermute(col, ('diag', 'tri'), [(b, a) for a, b in pairs])]
    gather x2 -> x0, local copies, waits for them, and re-layouts: 1.81 us -> none  [the longest x1 0.9 us: local(): picked_cols = jnp.take(held_block, tile_cols, axis=1)]
  transfers between devices with their start and end apart: 7 -> 2, of which waited for: 5 -> 0; matrix products, arithmetic and copies ran while one was open for 10% -> 0% of each run, Pallas kernels for 0% -> 10%
where the time goes in v1:
time: 71.3 us; the launch traced here: 70.8 us
  Pallas kernels  63.1 us (88%)
  local copies, waits for them, and re-layouts  4.71 us (7%)
  starting transfers between devices  2.3 us (3%)
  between operations  0.73 us (1%)
    pallas_call x1, Pallas kernels, reduced(): pl.pallas_call(reduce_kernel, out_shape=jax.ShapeDtypeStruct((columns, bl...  49.3 us
    pallas_call x2, Pallas kernels, product(): pl.pallas_call(functools.partial(product_kernel, transposed), out_shape=j...  13.7 us
    reshape x2, local copies, waits for them, and re-layouts, local(): trial_sets.transpose(1, 0, 2).reshape(columns, blocks, size)  1.84 us
    ppermute x1, starting transfers between devices, local(): back = lax.ppermute(col, ('diag', 'tri'), [(b, a) for a, b in pairs])  1.64 us
    reshape x1, local copies, waits for them, and re-layouts, local(): return out.reshape(vecs, sets, rows // tri).transpose(1, 0, 2)  1.45 us
    unnamed x6, local copies, waits for them, and re-layouts  1.43 us
  transfers between devices with their start and end apart: 2, of which 0 were waited for; matrix products, arithmetic and copies ran while one was open for 0% of the time, Pallas kernels for 10%

profile of v1, /device:TPU:1, one launch (start us, length us, event | category | flops | bytes accessed | tf_op | source)
XLA Modules:
  0.0 70.8 jit_solution(8638701602647768395)
XLA Ops:
  0.0 1.1 %reshape.6 = bf16[24,32,128]{2,1,0:T(8,128)(2,1)S(1)} reshape(bf16[12,2,4096]{2,1,0:T(2,128)(2,1)} %bitcast.11) | data formatting | bytes 393216 | tf_op jit(solution)/shard_map/reshape | solution.py:138
  1.1 0.8 %copy.7 = bf16[24,32,128]{2,0,1:T(8,128)(2,1)} copy(bf16[24,32,128]{2,1,0:T(8,128)(2,1)S(1)} %reshape.6) | data formatting | bytes 393216 | tf_op jit(solution)/shard_map/reshape | solution.py:138
  1.8 0.0 copy-start
  2.5 6.4 %col_product.1 = f32[32,24,128]{2,1,0:T(8,128)} custom-call(s32[2,192]{1,0:T(2,128)} %bitcast.12, s32[1,1]{1,0:T(1,128)S(6)} %copy.8.count, bf16[32,24,128]{2,1,0:T(8,128)(2,1)} %bitcast.9, bf16[192,128,128]{2,1,0:T(8,128)(2,1)} %bitcast.7), custom_call_target="tpu_custom_call" | custom-call | flops 150994944 | bytes 6881280 | tf_op jit(solution)/shard_map/col_product/pallas_call | solution.py:49
  9.0 1.6 %collective-permute-start.1 = (f32[32,24,128]{2,1,0:T(8,128)}, f32[32,24,128]{2,1,0:T(8,128)S(1)}, u32[]{:S(2)}, u32[]{:S(2)}) collective-permute-start(f32[32,24,128]{2,1,0:T(8,128)} %col_product.1), channel_id=1, source_target_pairs={{0,0},{9,1},{18,2},{27,3},{36,4},{45,5},{54,6},{63,7},{8,8},{17,9}... | collective-permute-start | bytes 1179656 | tf_op jit(solution)/shard_map/ppermute | solution.py:144
  10.6 0.0 copy-done
  10.6 0.7 collective-permute-start
  11.3 0.0 collective-permute-done.x_ref
  11.3 0.0 copy-start.2
  11.3 0.7 copy-done.2
  12.0 7.3 %row_product.1.row_ref = f32[32,24,128]{2,1,0:T(8,128)} custom-call(s32[2,192]{1,0:T(2,128)} %bitcast.13, s32[1,1]{1,0:T(1,128)S(6)} %copy.8.count, bf16[32,24,128]{2,1,0:T(8,128)(2,1)} %copy-done.2, bf16[192,128,128]{2,1,0:T(8,128)(2,1)} %bitcast.8), custom_call_target="tpu_custom_call" | custom-call | flops 150994944 | bytes 6881280 | tf_op jit(solution)/shard_map/row_product/pallas_call | solution.py:49
  19.3 0.0 collective-permute-done.1.col_ref
  19.3 0.0 copy-start.1
  19.3 0.8 %copy-done.1 = f32[32,24,128]{2,1,0:T(8,128)} copy-done((f32[32,24,128]{2,1,0:T(8,128)}, f32[32,24,128]{2,1,0:T(8,128)S(1)}, u32[]{:S(2)}) %copy-start.1) | copy-done | bytes 393240
  20.0 49.3 %reduce_tri.1 = f32[24,512]{1,0:T(8,128)} custom-call(f32[32,24,128]{2,1,0:T(8,128)} %row_product.1.row_ref, f32[32,24,128]{2,1,0:T(8,128)} %copy-done.1), custom_call_target="tpu_custom_call" | custom-call | tf_op jit(solution)/shard_map/reduce_tri/pallas_call | solution.py:114
  69.4 1.4 %reshape.7 = f32[12,2,512]{2,1,0:T(2,128)} reshape(f32[24,512]{1,0:T(8,128)} %reduce_tri.1) | data formatting | bytes 98304 | tf_op jit(solution)/shard_map/reshape | solution.py:147
Async XLA Ops:
  1.8 8.8 %copy-start = (bf16[24,32,128]{2,0,1:T(8,128)(2,1)S(1)}, bf16[24,32,128]{2,0,1:T(8,128)(2,1)}, u32[]{:S(2)}) copy-start(bf16[24,32,128]{2,0,1:T(8,128)(2,1)} %copy.7) | copy-start | bytes 589828
  9.0 10.3 %collective-permute-start.1 = (f32[32,24,128]{2,1,0:T(8,128)}, f32[32,24,128]{2,1,0:T(8,128)S(1)}, u32[]{:S(2)}, u32[]{:S(2)}) collective-permute-start(f32[32,24,128]{2,1,0:T(8,128)} %col_product.1), channel_id=1, source_target_pairs={{0,0},{9,1},{18,2},{27,3},{36,4},{45,5},{54,6},{63,7},{8,8},{17,9}... | collective-permute-start | bytes 1179656 | tf_op jit(solution)/shard_map/ppermute | solution.py:144
  10.6 0.7 collective-permute-start
  11.3 0.7 copy-start.2
  19.3 0.8 %copy-start.1 = (f32[32,24,128]{2,1,0:T(8,128)}, f32[32,24,128]{2,1,0:T(8,128)S(1)}, u32[]{:S(2)}) copy-start(f32[32,24,128]{2,1,0:T(8,128)S(1)} %collective-permute-done.1.col_ref) | copy-start | bytes 1179652

commit v2 on v0

v2 whole, which is shorter than its diff:
```python
import functools

import jax
import jax.numpy as jnp
from jax import lax
from jax.experimental import pallas as pl
from jax.experimental.pallas import tpu as pltpu
from jax.sharding import PartitionSpec as P

MESH = pl.DeviceIdType.MESH
UNROLL = 32
CHUNKS = 8


def depth(i, z_hi):
    return ((i >> 1) & 3) + 4 * z_hi


def near(i, z_hi, s, h):
    gap = (depth(i, z_hi) - depth(s, h)) & 7
    return (gap <= 1) | (gap == 7) | (gap == 2 + 4 * (i & 1))


def tables(pattern, live, place_first):
    rows, cols = pattern[0:1, :], pattern[1:2, :]
    target, source = (rows, cols) if place_first else (cols, rows)
    lane = lax.broadcasted_iota(jnp.int32, (1, 256), 1)
    placed = ((target >> 2) & 3) * 8 + (target >> 4) * 4 + (target & 3)
    word = placed * 8192 + source * 256 + lane
    word = word + jnp.where(lane < live, 0, 1 << 18)
    word = jnp.where(lane < 192, word, (1 << 20) + lane)

    def column(row):
        wide = jnp.broadcast_to(row, (128, 256))
        tall = jnp.concatenate([wide[:, :128].T, wide[:, 128:].T], 0)
        return jnp.concatenate([tall, tall], 1)

    tall = column(word)
    rank = jnp.sum(jnp.where(tall < word, 1, 0), axis=0, keepdims=True)
    spot = column(rank)
    order = jnp.sum(jnp.where(spot == lane, tall, 0), axis=0, keepdims=True)
    below = jnp.sum(jnp.where(tall < (lane + 1) * 8192, 1, 0), axis=0, keepdims=True)
    before = jnp.sum(jnp.where(tall < lane * 8192, 1, 0), axis=0, keepdims=True)
    ends = jnp.where(below == before, 192, below - 1)
    return order, ends


def visit(transposed, row, first, last, acc, table, tiles, xs, runs):
    contract = (((1,), (1,)), ((), ())) if transposed else (((1,), (0,)), ((), ()))
    side = 0 if transposed else 1

    def body(step, acc):
        base = step * UNROLL
        words = [table[row, base + u] for u in range(UNROLL)]
        terms = []
        for u in range(0, UNROLL, 2):
            pair = words[u : u + 2]
            left = jnp.concatenate([xs[(w >> 8) & 31] for w in pair], 0)
            right = jnp.concatenate([tiles[w & 255] for w in pair], side)
            both = lax.dot_general(left, right, contract, preferred_element_type=jnp.float32)
            terms += [both[0:24, 0:128], both[24:48, 128:256]]
        past = table[row, jnp.maximum(base - 1, 0)]
        for u in range(UNROLL):
            same = (words[u] >> 13) == (past >> 13)
            past = words[u]
            acc = terms[u] + jnp.where(same, acc, 0.0)
            runs[base + u] = acc
        return acc

    return lax.fori_loop(first, last, body, acc)


def kernel(
    x_hbm, pattern_hbm, count, tiles_hbm, out_ref,
    raw, pattern, padded, table_v, table, tiles, own, held, runs,
    col, row, col_got, x_got, half, half_got,
    load, tile_sem, x_send, x_recv, col_send, col_recv, row_send, row_recv, z_sem,
):
    i, k = lax.axis_index("diag"), lax.axis_index("tri")
    x, z_hi = k & 3, k >> 2
    source = (i - k) & 31
    home = k == 0
    from_half = jnp.where(near(i, z_hi, source, 0), 0, 1)
    giver = {"diag": source, "tri": from_half * 4 + x}
    takers = []
    for h in (0, 1):
        user = (i + 4 * h + x) & 31
        takes = near(user, h, i, z_hi) & jnp.logical_not((h * 4 + x) == 0)
        takers.append((takes, {"diag": user, "tri": h * 4 + x}))
    peers = [{"diag": i, "tri": z_hi * 4 + ((x + d) & 3)} for d in (1, 2, 3)]
    across = {"diag": i, "tri": k ^ 4}

    barrier = pltpu.get_barrier_semaphore()
    expected = jnp.int32(4)
    for peer in [across, *peers]:
        pl.semaphore_signal(barrier, inc=1, device_id=peer, device_id_type=MESH)
    for takes, user in [*takers, (jnp.logical_not(home), giver)]:
        expected = expected + takes.astype(jnp.int32)

        @pl.when(takes)
        def _():
            pl.semaphore_signal(barrier, inc=1, device_id=user, device_id_type=MESH)

    get_pattern = pltpu.make_async_copy(pattern_hbm, pattern, load.at[0])
    get_x = pltpu.make_async_copy(x_hbm, raw, load.at[1])
    get_pattern.start()
    get_x.start()
    each = 192 // CHUNKS
    get_tiles = []
    for n in range(CHUNKS):
        part = pl.ds(n * each, each)
        get_tiles.append(pltpu.make_async_copy(tiles_hbm.at[part], tiles.at[part], tile_sem.at[n]))
        get_tiles[n].start()

    get_pattern.wait()
    padded[:, 0:192] = pattern[...]
    padded[:, 192:256] = jnp.zeros((2, 64), jnp.int32)
    slots = padded[...]
    live = count[0, 0]
    col_order, col_ends = tables(slots, live, False)
    row_order, row_ends = tables(slots, live, True)
    table_v[...] = jnp.concatenate([col_order, col_ends, row_order, row_ends] * 2, 0)
    runs[192] = jnp.zeros((24, 128), jnp.float32)

    get_x.wait()
    whole = jnp.concatenate([raw[p] for p in range(12)], 0)
    for c in range(32):
        own[c] = whole[:, c * 128 : (c + 1) * 128]
    get_table = pltpu.make_async_copy(table_v, table, load.at[2])
    get_table.start()
    get_table.wait()

    for copy in get_tiles:
        copy.wait()
    acc = jnp.zeros((24, 128), jnp.float32)
    acc = visit(False, 0, 0, 2, acc, table, tiles, own, runs)

    pl.semaphore_wait(barrier, expected)
    give = []
    for h in (0, 1):
        takes, user = takers[h]
        copy = pltpu.make_async_remote_copy(own, held, x_send.at[h], x_recv, device_id=user, device_id_type=MESH)
        give.append(copy)

        @pl.when(takes)
        def _():
            copy.start()

    keep = pltpu.make_async_copy(own, held, x_recv)

    @pl.when(home)
    def _():
        keep.start()

    acc = visit(False, 0, 2, 192 // UNROLL, acc, table, tiles, own, runs)
    for p in range(32):
        col[p] = runs[table[1, p]]

    back = pltpu.make_async_remote_copy(
        col, col_got.at[z_hi], col_send, col_recv.at[z_hi], device_id=giver, device_id_type=MESH
    )

    @pl.when(jnp.logical_not(home))
    def _():
        back.start()
        pltpu.make_async_remote_copy(own, held, x_send.at[0], x_recv, device_id=giver, device_id_type=MESH).wait_recv()

    @pl.when(home)
    def _():
        keep.wait()

    acc = jnp.zeros((24, 128), jnp.float32)
    visit(True, 2, 0, 192 // UNROLL, acc, table, tiles, held, runs)
    for p in range(32):
        row[p] = runs[table[3, p]]

    @pl.when(home)
    def _():
        row[...] += col[...]

    for h in (0, 1):
        takes, user = takers[h]

        @pl.when(takes)
        def _():
            pltpu.make_async_remote_copy(
                col, col_got.at[h], col_send, col_recv.at[h], device_id=user, device_id_type=MESH
            ).wait_recv()
            row[...] += col_got[h]

    scatter = []
    for d in (2, 1, 3):
        to = (x + d) & 3
        copy = pltpu.make_async_remote_copy(
            row.at[pl.ds(to * 8, 8)],
            x_got.at[d - 1],
            row_send.at[d - 1],
            row_recv.at[d - 1],
            device_id={"diag": i, "tri": z_hi * 4 + to},
            device_id_type=MESH,
        )
        copy.start()
        scatter.append(copy)

    for h in (0, 1):
        takes, user = takers[h]

        @pl.when(takes)
        def _():
            give[h].wait_send()

    @pl.when(jnp.logical_not(home))
    def _():
        back.wait_send()

    for copy in scatter:
        copy.wait_recv()
    for n, side in enumerate((1 - z_hi, z_hi)):
        total = row[pl.ds(x * 8 + side * 4, 4)]
        for d in range(3):
            total = total + x_got[d, pl.ds(side * 4, 4)]
        half[n] = total
    swap = pltpu.make_async_remote_copy(
        half.at[0], half_got, z_sem.at[0], z_sem.at[1], device_id=across, device_id_type=MESH
    )
    swap.start()
    for copy in scatter:
        copy.wait_send()
    swap.wait()
    for j in range(4):
        out_ref[:, j * 128 : (j + 1) * 128] = half[1, j] + half_got[j]


def local(trial_sets, tile_values, tile_pattern, tile_count):
    sets, vecs, rows = trial_sets.shape
    tri = lax.axis_size("tri")
    columns = sets * vecs
    slots, size = tile_values.shape[2:4]
    blocks = rows // size
    f32, bf16, i32 = jnp.float32, jnp.bfloat16, jnp.int32
    dma = pltpu.SemaphoreType.DMA
    block = (columns, size)
    out = pl.pallas_call(
        kernel,
        out_shape=jax.ShapeDtypeStruct((columns, rows // tri), f32),
        in_specs=[
            pl.BlockSpec(memory_space=pl.ANY),
            pl.BlockSpec(memory_space=pl.ANY),
            pl.BlockSpec(memory_space=pltpu.SMEM),
            pl.BlockSpec(memory_space=pl.ANY),
        ],
        out_specs=pl.BlockSpec(memory_space=pltpu.VMEM),
        scratch_shapes=[
            pltpu.VMEM((vecs, sets, rows), bf16),
            pltpu.VMEM((2, slots), i32),
            pltpu.VMEM((2, 256), i32),
            pltpu.VMEM((8, 256), i32),
            pltpu.SMEM((8, 256), i32),
            pltpu.VMEM((slots, size, size), bf16),
            pltpu.VMEM((blocks, *block), bf16),
            pltpu.VMEM((blocks, *block), bf16),
            pltpu.VMEM((slots + 8, *block), f32),
            pltpu.VMEM((blocks, *block), f32),
            pltpu.VMEM((blocks, *block), f32),
            pltpu.VMEM((2, blocks, *block), f32),
            pltpu.VMEM((3, 8, *block), f32),
            pltpu.VMEM((2, 4, *block), f32),
            pltpu.VMEM((4, *block), f32),
            dma((3,)),
            dma((CHUNKS,)),
            dma((2,)),
            dma(()),
            dma(()),
            dma((2,)),
            dma((3,)),
            dma((3,)),
            dma((2,)),
        ],
        compiler_params=pltpu.CompilerParams(
            collective_id=0, has_side_effects=True, vmem_limit_bytes=63 << 20
        ),
        name="block_products",
    )(trial_sets.transpose(1, 0, 2), tile_pattern[0, 0], tile_count, tile_values[0, 0])
    return out.reshape(vecs, sets, rows // tri).transpose(1, 0, 2)


def solution(mesh):
    return jax.shard_map(
        local,
        mesh=mesh,
        in_specs=(
            P(None, None, "diag"),
            P("diag", "tri", None, None, None),
            P("diag", "tri", None, None),
            P("diag", "tri"),
        ),
        out_specs=P(None, None, ("diag", "tri")),
        check_vma=False,
    )
```

time: 168 us -> 40.7 us (0.24)
  the two profiles are of different devices: /device:TPU:1 before, /device:TPU:104 now
where the time goes in v2:
time: 40.7 us; the launch traced here: 40.5 us
  Pallas kernels  38.4 us (94%)
  local copies, waits for them, and re-layouts  1.45 us (4%)
  between operations  0.66 us (2%)
    pallas_call x1, Pallas kernels, local(): pl.pallas_call(kernel, out_shape=jax.ShapeDtypeStruct((columns, rows // t...  38.4 us
    reshape x1, local copies, waits for them, and re-layouts, local(): return out.reshape(vecs, sets, rows // tri).transpose(1, 0, 2)  1.45 us

profile of v2, /device:TPU:104, one launch (start us, length us, event | category | flops | bytes accessed | tf_op | source)
XLA Modules:
  0.0 40.5 jit_solution(14425241141085205661)
XLA Ops:
  0.7 38.4 %block_products.1 = f32[24,512]{1,0:T(8,128)} custom-call(bf16[12,2,4096]{2,1,0:T(2,128)(2,1)} %bitcast.5, s32[2,192]{1,0:T(2,128)} %bitcast.6, s32[1,1]{1,0:T(1,128)S(6)} %copy.5.count, bf16[192,128,128]{2,1,0:T(8,128)(2,1)} %bitcast.4), custom_call_target="tpu_custom_call" | custom-call | tf_op jit(solution)/shard_map/block_products/pallas_call | solution.py:243
  39.1 1.4 %reshape.3 = f32[12,2,512]{2,1,0:T(2,128)} reshape(f32[24,512]{1,0:T(8,128)} %block_products.1) | data formatting | bytes 98304 | tf_op jit(solution)/shard_map/reshape | solution.py:284

commit v3 on v2

--- a/solution.py
+++ b/solution.py
@@ -12,13 +12,12 @@
 CHUNKS = 8
 
 
-def depth(i, z_hi):
-    return ((i >> 1) & 3) + 4 * z_hi
-
-
-def near(i, z_hi, s, h):
-    gap = (depth(i, z_hi) - depth(s, h)) & 7
-    return (gap <= 1) | (gap == 7) | (gap == 2 + 4 * (i & 1))
+HALVES = (0x2822, 0x8A23, 0x08AB, 0x23AE)
+
+
+def half_of(i, z_hi, x):
+    bits = jnp.where(x < 2, jnp.where(x == 0, HALVES[0], HALVES[1]), jnp.where(x == 2, HALVES[2], HALVES[3]))
+    return (bits >> ((i & 7) * 2 + z_hi)) & 1
 
 
 def tables(pattern, live, place_first):
@@ -43,6 +42,11 @@
     before = jnp.sum(jnp.where(tall < lane * 8192, 1, 0), axis=0, keepdims=True)
     ends = jnp.where(below == before, 192, below - 1)
     return order, ends
+
+
+def coded(value):
+    scale = jnp.maximum(jnp.max(jnp.abs(value), axis=1, keepdims=True), 4e-34)
+    return jnp.round(value * (32767.0 / scale)).astype(jnp.int32).astype(jnp.int16), scale * (1 / 32767.0)
 
 
 def visit(transposed, row, first, last, acc, table, tiles, xs, runs):
@@ -73,19 +77,19 @@
 def kernel(
     x_hbm, pattern_hbm, count, tiles_hbm, out_ref,
     raw, pattern, padded, table_v, table, tiles, own, held, runs,
-    col, row, col_got, x_got, half, half_got,
-    load, tile_sem, x_send, x_recv, col_send, col_recv, row_send, row_recv, z_sem,
+    col, col_scale, row, col_got, scale_got, x_got, half, half_got,
+    load, tile_sem, x_send, x_recv, col_send, col_recv, scale_send, scale_recv, row_send, row_recv, z_sem,
 ):
     i, k = lax.axis_index("diag"), lax.axis_index("tri")
     x, z_hi = k & 3, k >> 2
     source = (i - k) & 31
     home = k == 0
-    from_half = jnp.where(near(i, z_hi, source, 0), 0, 1)
+    from_half = half_of(i, z_hi, x)
     giver = {"diag": source, "tri": from_half * 4 + x}
     takers = []
     for h in (0, 1):
         user = (i + 4 * h + x) & 31
-        takes = near(user, h, i, z_hi) & jnp.logical_not((h * 4 + x) == 0)
+        takes = (half_of(user, h, x) == z_hi) & jnp.logical_not((h * 4 + x) == 0)
         takers.append((takes, {"diag": user, "tri": h * 4 + x}))
     peers = [{"diag": i, "tri": z_hi * 4 + ((x + d) & 3)} for d in (1, 2, 3)]
     across = {"diag": i, "tri": k ^ 4}
@@ -153,16 +157,26 @@
         keep.start()
 
     acc = visit(False, 0, 2, 192 // UNROLL, acc, table, tiles, own, runs)
+    lane = lax.broadcasted_iota(jnp.int32, (24, 128), 1)
+    scales = jnp.zeros((24, 128), jnp.float32)
     for p in range(32):
-        col[p] = runs[table[1, p]]
-
-    back = pltpu.make_async_remote_copy(
-        col, col_got.at[z_hi], col_send, col_recv.at[z_hi], device_id=giver, device_id_type=MESH
-    )
+        col[p], scale = coded(runs[table[1, p]])
+        scales = jnp.where(lane == p, scale, scales)
+    col_scale[...] = scales
+
+    back = [
+        pltpu.make_async_remote_copy(
+            col, col_got.at[z_hi], col_send, col_recv.at[z_hi], device_id=giver, device_id_type=MESH
+        ),
+        pltpu.make_async_remote_copy(
+            col_scale, scale_got.at[z_hi], scale_send, scale_recv.at[z_hi], device_id=giver, device_id_type=MESH
+        ),
+    ]
 
     @pl.when(jnp.logical_not(home))
     def _():
-        back.start()
+        for copy in back:
+            copy.start()
         pltpu.make_async_remote_copy(own, held, x_send.at[0], x_recv, device_id=giver, device_id_type=MESH).wait_recv()
 
     @pl.when(home)
@@ -174,9 +188,14 @@
     for p in range(32):
         row[p] = runs[table[3, p]]
 
+    def add(codes, scale):
+        scale = scale[...]
+        for p in range(32):
+            row[p] += codes[p].astype(jnp.int32).astype(jnp.float32) * scale[:, p : p + 1]
+
     @pl.when(home)
     def _():
-        row[...] += col[...]
+        add(col, col_scale)
 
     for h in (0, 1):
         takes, user = takers[h]
@@ -186,7 +205,10 @@
             pltpu.make_async_remote_copy(
                 col, col_got.at[h], col_send, col_recv.at[h], device_id=user, device_id_type=MESH
             ).wait_recv()
-            row[...] += col_got[h]
+            pltpu.make_async_remote_copy(
+                col_scale, scale_got.at[h], scale_send, scale_recv.at[h], device_id=user, device_id_type=MESH
+            ).wait_recv()
+            add(col_got.at[h], scale_got.at[h])
 
     scatter = []
     for d in (2, 1, 3):
@@ -211,7 +233,8 @@
 
     @pl.when(jnp.logical_not(home))
     def _():
-        back.wait_send()
+        for copy in back:
+            copy.wait_send()
 
     for copy in scatter:
         copy.wait_recv()
@@ -228,7 +251,9 @@
         copy.wait_send()
     swap.wait()
     for j in range(4):
-        out_ref[:, j * 128 : (j + 1) * 128] = half[1, j] + half_got[j]
+        total = half[1, j] + half_got[j]
+        for p in range(12):
+            out_ref[p, :, j * 128 : (j + 1) * 128] = total[2 * p : 2 * p + 2, :]
 
 
 def local(trial_sets, tile_values, tile_pattern, tile_count):
@@ -242,7 +267,7 @@
     block = (columns, size)
     out = pl.pallas_call(
         kernel,
-        out_shape=jax.ShapeDtypeStruct((columns, rows // tri), f32),
+        out_shape=jax.ShapeDtypeStruct((vecs, sets, rows // tri), f32),
         in_specs=[
             pl.BlockSpec(memory_space=pl.ANY),
             pl.BlockSpec(memory_space=pl.ANY),
@@ -260,9 +285,11 @@
             pltpu.VMEM((blocks, *block), bf16),
             pltpu.VMEM((blocks, *block), bf16),
             pltpu.VMEM((slots + 8, *block), f32),
+            pltpu.VMEM((blocks, *block), jnp.int16),
+            pltpu.VMEM(block, f32),
             pltpu.VMEM((blocks, *block), f32),
-            pltpu.VMEM((blocks, *block), f32),
-            pltpu.VMEM((2, blocks, *block), f32),
+            pltpu.VMEM((2, blocks, *block), jnp.int16),
+            pltpu.VMEM((2, *block), f32),
             pltpu.VMEM((3, 8, *block), f32),
             pltpu.VMEM((2, 4, *block), f32),
             pltpu.VMEM((4, *block), f32),
@@ -270,6 +297,8 @@
             dma((CHUNKS,)),
             dma((2,)),
             dma(()),
+            dma(()),
+            dma((2,)),
             dma(()),
             dma((2,)),
             dma((3,)),
@@ -281,7 +310,7 @@
         ),
         name="block_products",
     )(trial_sets.transpose(1, 0, 2), tile_pattern[0, 0], tile_count, tile_values[0, 0])
-    return out.reshape(vecs, sets, rows // tri).transpose(1, 0, 2)
+    return out.transpose(1, 0, 2)
 
 
 def solution(mesh):

time: 40.7 us -> 37.4 us (0.919)
  the two profiles are of different devices: /device:TPU:104 before, /device:TPU:2 now
where the time goes in v3:
time: 37.4 us; the launch traced here: 37.3 us
  Pallas kernels  35.2 us (94%)
  local copies, waits for them, and re-layouts  1.42 us (4%)
  between operations  0.66 us (2%)
    pallas_call x1, Pallas kernels, local(): pl.pallas_call(kernel, out_shape=jax.ShapeDtypeStruct((vecs, sets, rows /...  35.2 us
    unnamed x1, local copies, waits for them, and re-layouts  1.42 us

profile of v3, /device:TPU:2, one launch (start us, length us, event | category | flops | bytes accessed | tf_op | source)
XLA Modules:
  0.0 37.3 jit_solution(10099184018872015226)
XLA Ops:
  0.7 35.2 %block_products.1 = f32[12,2,512]{2,1,0:T(2,128)} custom-call(bf16[12,2,4096]{2,1,0:T(2,128)(2,1)} %bitcast.6, s32[2,192]{1,0:T(2,128)} %bitcast.7, s32[1,1]{1,0:T(1,128)S(6)} %copy.6.count, bf16[192,128,128]{2,1,0:T(8,128)(2,1)} %bitcast.4), custom_call_target="tpu_custom_call" | custom-call | tf_op jit(solution)/shard_map/block_products/pallas_call | solution.py:268
  35.8 1.4 %copy.7 = f32[2,12,512]{2,0,1:T(2,128)} copy(f32[2,12,512]{2,0,1:T(2,128)} %bitcast.5) | data formatting | bytes 98304

commit v4 on v3

--- a/solution.py
+++ b/solution.py
@@ -24,8 +24,7 @@
     rows, cols = pattern[0:1, :], pattern[1:2, :]
     target, source = (rows, cols) if place_first else (cols, rows)
     lane = lax.broadcasted_iota(jnp.int32, (1, 256), 1)
-    placed = ((target >> 2) & 3) * 8 + (target >> 4) * 4 + (target & 3)
-    word = placed * 8192 + source * 256 + lane
+    word = target * 8192 + source * 256 + lane
     word = word + jnp.where(lane < live, 0, 1 << 18)
     word = jnp.where(lane < 192, word, (1 << 20) + lane)
 
@@ -44,16 +43,20 @@
     return order, ends
 
 
-def coded(value):
-    scale = jnp.maximum(jnp.max(jnp.abs(value), axis=1, keepdims=True), 4e-34)
-    return jnp.round(value * (32767.0 / scale)).astype(jnp.int32).astype(jnp.int16), scale * (1 / 32767.0)
-
-
-def visit(transposed, row, first, last, acc, table, tiles, xs, runs):
+def coded(values):
+    most = functools.reduce(jnp.maximum, [jnp.abs(v) for v in values])
+    scale = jnp.maximum(jnp.max(most, axis=1, keepdims=True), 4e-34)
+    grow = jnp.broadcast_to(32767.0 / scale, most.shape)
+    return [jnp.round(v * grow).astype(jnp.int32).astype(jnp.int16) for v in values], scale * (1 / 32767.0)
+
+
+def visit(transposed, row, first, last, acc, table, tiles, xs, runs, meet=None):
     contract = (((1,), (1,)), ((), ())) if transposed else (((1,), (0,)), ((), ()))
     side = 0 if transposed else 1
 
     def body(step, acc):
+        if meet:
+            meet(step)
         base = step * UNROLL
         words = [table[row, base + u] for u in range(UNROLL)]
         terms = []
@@ -77,8 +80,8 @@
 def kernel(
     x_hbm, pattern_hbm, count, tiles_hbm, out_ref,
     raw, pattern, padded, table_v, table, tiles, own, held, runs,
-    col, col_scale, row, col_got, scale_got, x_got, half, half_got,
-    load, tile_sem, x_send, x_recv, col_send, col_recv, scale_send, scale_recv, row_send, row_recv, z_sem,
+    col, col_scale, row, col_got, scale_got, pieces,
+    load, tile_sem, x_send, x_recv, col_send, col_recv, scale_send, scale_recv, row_send, row_recv,
 ):
     i, k = lax.axis_index("diag"), lax.axis_index("tri")
     x, z_hi = k & 3, k >> 2
@@ -91,19 +94,7 @@
         user = (i + 4 * h + x) & 31
         takes = (half_of(user, h, x) == z_hi) & jnp.logical_not((h * 4 + x) == 0)
         takers.append((takes, {"diag": user, "tri": h * 4 + x}))
-    peers = [{"diag": i, "tri": z_hi * 4 + ((x + d) & 3)} for d in (1, 2, 3)]
-    across = {"diag": i, "tri": k ^ 4}
-
-    barrier = pltpu.get_barrier_semaphore()
-    expected = jnp.int32(4)
-    for peer in [across, *peers]:
-        pl.semaphore_signal(barrier, inc=1, device_id=peer, device_id_type=MESH)
-    for takes, user in [*takers, (jnp.logical_not(home), giver)]:
-        expected = expected + takes.astype(jnp.int32)
-
-        @pl.when(takes)
-        def _():
-            pl.semaphore_signal(barrier, inc=1, device_id=user, device_id_type=MESH)
+    peers = [((1 - z_hi) * 4 + ((x + d) & 3)) for d in (2, 1, 3, 0)] + [z_hi * 4 + ((x + d) & 3) for d in (2, 1, 3)]
 
     get_pattern = pltpu.make_async_copy(pattern_hbm, pattern, load.at[0])
     get_x = pltpu.make_async_copy(x_hbm, raw, load.at[1])
@@ -116,20 +107,33 @@
         get_tiles.append(pltpu.make_async_copy(tiles_hbm.at[part], tiles.at[part], tile_sem.at[n]))
         get_tiles[n].start()
 
-    get_pattern.wait()
-    padded[:, 0:192] = pattern[...]
-    padded[:, 192:256] = jnp.zeros((2, 64), jnp.int32)
-    slots = padded[...]
-    live = count[0, 0]
-    col_order, col_ends = tables(slots, live, False)
-    row_order, row_ends = tables(slots, live, True)
-    table_v[...] = jnp.concatenate([col_order, col_ends, row_order, row_ends] * 2, 0)
-    runs[192] = jnp.zeros((24, 128), jnp.float32)
+    barrier = pltpu.get_barrier_semaphore()
+    expected = jnp.int32(7)
+    for takes, user in [*takers, (jnp.logical_not(home), giver)]:
+        expected = expected + takes.astype(jnp.int32)
+
+        @pl.when(takes)
+        def _():
+            pl.semaphore_signal(barrier, inc=1, device_id=user, device_id_type=MESH)
+    for peer in peers:
+        pl.semaphore_signal(barrier, inc=1, device_id={"diag": i, "tri": peer}, device_id_type=MESH)
 
     get_x.wait()
     whole = jnp.concatenate([raw[p] for p in range(12)], 0)
     for c in range(32):
         own[c] = whole[:, c * 128 : (c + 1) * 128]
+    get_pattern.wait()
+    padded[:, 0:192] = pattern[...]
+    padded[:, 192:256] = jnp.zeros((2, 64), jnp.int32)
+    pairs = padded[...]
+    live = count[0, 0]
+    col_order, col_ends = tables(pairs, live, False)
+    row_order, row_ends = tables(pairs, live, True)
+    table_v[...] = jnp.concatenate([col_order, col_ends, row_order, row_ends] * 2, 0)
+    runs[192] = jnp.zeros((24, 128), jnp.float32)
+    col_got[2] = jnp.zeros((32, 24, 128), jnp.int16)
+    scale_got[2] = jnp.zeros((24, 128), jnp.float32)
+
     get_table = pltpu.make_async_copy(table_v, table, load.at[2])
     get_table.start()
     get_table.wait()
@@ -137,31 +141,31 @@
     for copy in get_tiles:
         copy.wait()
     acc = jnp.zeros((24, 128), jnp.float32)
-    acc = visit(False, 0, 0, 2, acc, table, tiles, own, runs)
-
-    pl.semaphore_wait(barrier, expected)
+    meeting = jnp.where(z_hi == 0, jnp.maximum(2 - ((i >> 1) & 3), 0), 0)
     give = []
     for h in (0, 1):
         takes, user = takers[h]
-        copy = pltpu.make_async_remote_copy(own, held, x_send.at[h], x_recv, device_id=user, device_id_type=MESH)
-        give.append(copy)
-
-        @pl.when(takes)
+        give.append(
+            pltpu.make_async_remote_copy(own, held, x_send.at[h], x_recv, device_id=user, device_id_type=MESH)
+        )
+    keep = pltpu.make_async_copy(own, held, x_recv)
+
+    def meet(step):
+        @pl.when(step == meeting)
         def _():
-            copy.start()
-
-    keep = pltpu.make_async_copy(own, held, x_recv)
-
-    @pl.when(home)
-    def _():
-        keep.start()
-
-    acc = visit(False, 0, 2, 192 // UNROLL, acc, table, tiles, own, runs)
+            pl.semaphore_wait(barrier, expected)
+            for h in (0, 1):
+                pl.when(takers[h][0])(give[h].start)
+            pl.when(home)(keep.start)
+
+    visit(False, 0, 0, 192 // UNROLL, acc, table, tiles, own, runs, meet)
     lane = lax.broadcasted_iota(jnp.int32, (24, 128), 1)
     scales = jnp.zeros((24, 128), jnp.float32)
-    for p in range(32):
-        col[p], scale = coded(runs[table[1, p]])
-        scales = jnp.where(lane == p, scale, scales)
+    for t in range(8):
+        codes, scale = coded([runs[table[1, t * 4 + j]] for j in range(4)])
+        for j in range(4):
+            col[t * 4 + j] = codes[j]
+        scales = jnp.where(lane == t, scale, scales)
     col_scale[...] = scales
 
     back = [
@@ -179,26 +183,26 @@
             copy.start()
         pltpu.make_async_remote_copy(own, held, x_send.at[0], x_recv, device_id=giver, device_id_type=MESH).wait_recv()
 
+    keep_col = pltpu.make_async_copy(col, col_got.at[0], col_recv.at[0])
+    keep_scale = pltpu.make_async_copy(col_scale, scale_got.at[0], scale_recv.at[0])
+
     @pl.when(home)
     def _():
+        keep_col.start()
+        keep_scale.start()
         keep.wait()
 
-    acc = jnp.zeros((24, 128), jnp.float32)
     visit(True, 2, 0, 192 // UNROLL, acc, table, tiles, held, runs)
-    for p in range(32):
-        row[p] = runs[table[3, p]]
-
-    def add(codes, scale):
-        scale = scale[...]
-        for p in range(32):
-            row[p] += codes[p].astype(jnp.int32).astype(jnp.float32) * scale[:, p : p + 1]
-
     @pl.when(home)
     def _():
-        add(col, col_scale)
-
+        keep_col.wait()
+        keep_scale.wait()
+
+    slots = []
     for h in (0, 1):
         takes, user = takers[h]
+        filled = takes if h else takes | home
+        slots.append(jnp.where(filled, h, 2))
 
         @pl.when(takes)
         def _():
@@ -208,17 +212,26 @@
             pltpu.make_async_remote_copy(
                 col_scale, scale_got.at[h], scale_send, scale_recv.at[h], device_id=user, device_id_type=MESH
             ).wait_recv()
-            add(col_got.at[h], scale_got.at[h])
 
     scatter = []
-    for d in (2, 1, 3):
-        to = (x + d) & 3
+    scales = [scale_got[slot] for slot in slots]
+    for n, peer in enumerate([*peers, k]):
+        part = [jnp.sum(jnp.where(lane == peer, s, 0.0), axis=1, keepdims=True) for s in scales]
+        part = [jnp.broadcast_to(s, (24, 128)) for s in part]
+        for j in range(4):
+            p = peer * 4 + j
+            total = runs[table[3, p]]
+            for slot, scale in zip(slots, part):
+                total = total + col_got[slot, p].astype(jnp.int32).astype(jnp.float32) * scale
+            row[p] = total
+        if n == 7:
+            break
         copy = pltpu.make_async_remote_copy(
-            row.at[pl.ds(to * 8, 8)],
-            x_got.at[d - 1],
-            row_send.at[d - 1],
-            row_recv.at[d - 1],
-            device_id={"diag": i, "tri": z_hi * 4 + to},
+            row.at[pl.ds(peer * 4, 4)],
+            pieces.at[n],
+            row_send.at[n],
+            row_recv.at[n],
+            device_id={"diag": i, "tri": peer},
             device_id_type=MESH,
         )
         copy.start()
@@ -237,21 +250,11 @@
             copy.wait_send()
 
     for copy in scatter:
-        copy.wait_recv()
-    for n, side in enumerate((1 - z_hi, z_hi)):
-        total = row[pl.ds(x * 8 + side * 4, 4)]
-        for d in range(3):
-            total = total + x_got[d, pl.ds(side * 4, 4)]
-        half[n] = total
-    swap = pltpu.make_async_remote_copy(
-        half.at[0], half_got, z_sem.at[0], z_sem.at[1], device_id=across, device_id_type=MESH
-    )
-    swap.start()
-    for copy in scatter:
-        copy.wait_send()
-    swap.wait()
+        copy.wait()
     for j in range(4):
-        total = half[1, j] + half_got[j]
+        total = row[k * 4 + j]
+        for n in range(7):
+            total = total + pieces[n, j]
         for p in range(12):
             out_ref[p, :, j * 128 : (j + 1) * 128] = total[2 * p : 2 * p + 2, :]
 
@@ -288,11 +291,9 @@
             pltpu.VMEM((blocks, *block), jnp.int16),
             pltpu.VMEM(block, f32),
             pltpu.VMEM((blocks, *block), f32),
-            pltpu.VMEM((2, blocks, *block), jnp.int16),
-            pltpu.VMEM((2, *block), f32),
-            pltpu.VMEM((3, 8, *block), f32),
-            pltpu.VMEM((2, 4, *block), f32),
-            pltpu.VMEM((4, *block), f32),
+            pltpu.VMEM((3, blocks, *block), jnp.int16),
+            pltpu.VMEM((3, *block), f32),
+            pltpu.VMEM((7, 4, *block), f32),
             dma((3,)),
             dma((CHUNKS,)),
             dma((2,)),
@@ -301,9 +302,8 @@
             dma((2,)),
             dma(()),
             dma((2,)),
-            dma((3,)),
-            dma((3,)),
-            dma((2,)),
+            dma((7,)),
+            dma((7,)),
         ],
         compiler_params=pltpu.CompilerParams(
             collective_id=0, has_side_effects=True, vmem_limit_bytes=63 << 20

time: 37.4 us -> 34.2 us (0.914)
  the two profiles are of different devices: /device:TPU:2 before, /device:TPU:24 now
where the time goes in v4:
time: 34.2 us; the launch traced here: 34.1 us
  Pallas kernels  32 us (94%)
  local copies, waits for them, and re-layouts  1.42 us (4%)
  between operations  0.66 us (2%)
    pallas_call x1, Pallas kernels, local(): pl.pallas_call(kernel, out_shape=jax.ShapeDtypeStruct((vecs, sets, rows /...  32 us
    unnamed x1, local copies, waits for them, and re-layouts  1.42 us

profile of v4, /device:TPU:24, one launch (start us, length us, event | category | flops | bytes accessed | tf_op | source)
XLA Modules:
  0.0 34.1 jit_solution(13045362614115401393)
XLA Ops:
  0.7 32.0 %block_products.1 = f32[12,2,512]{2,1,0:T(2,128)} custom-call(bf16[12,2,4096]{2,1,0:T(2,128)(2,1)} %bitcast.6, s32[2,192]{1,0:T(2,128)} %bitcast.7, s32[1,1]{1,0:T(1,128)S(6)} %copy.6.count, bf16[192,128,128]{2,1,0:T(8,128)(2,1)} %bitcast.4), custom_call_target="tpu_custom_call" | custom-call | tf_op jit(solution)/shard_map/block_products/pallas_call | solution.py:271
  32.7 1.4 %copy.7 = f32[2,12,512]{2,0,1:T(2,128)} copy(f32[2,12,512]{2,0,1:T(2,128)} %bitcast.5) | data formatting | bytes 98304

commit v5 on v4

--- a/solution.py
+++ b/solution.py
@@ -8,7 +8,8 @@
 from jax.sharding import PartitionSpec as P
 
 MESH = pl.DeviceIdType.MESH
-UNROLL = 32
+COL_UNROLL = 32
+ROW_UNROLL = 48
 CHUNKS = 8
 
 
@@ -50,9 +51,23 @@
     return [jnp.round(v * grow).astype(jnp.int32).astype(jnp.int16) for v in values], scale * (1 / 32767.0)
 
 
+def packed(values):
+    most = functools.reduce(jnp.maximum, [jnp.abs(v) for v in values])
+    scale = jnp.maximum(jnp.max(most, axis=1, keepdims=True), 4e-34)
+    level = jnp.broadcast_to(jnp.ceil(jnp.log2(scale) * 128.0), most.shape)
+    grow = 32700.0 / jnp.exp2(level * (1 / 128.0))
+    return [v.astype(jnp.int32).astype(jnp.int16) for v in [*(jnp.round(v * grow) for v in values), level]]
+
+
+def unpacked(codes):
+    scale = jnp.exp2(codes[4].astype(jnp.int32).astype(jnp.float32) * (1 / 128.0)) * (1 / 32700.0)
+    return [codes[j].astype(jnp.int32).astype(jnp.float32) * scale for j in range(4)]
+
+
 def visit(transposed, row, first, last, acc, table, tiles, xs, runs, meet=None):
     contract = (((1,), (1,)), ((), ())) if transposed else (((1,), (0,)), ((), ()))
     side = 0 if transposed else 1
+    UNROLL = ROW_UNROLL if transposed else COL_UNROLL
 
     def body(step, acc):
         if meet:
@@ -80,7 +95,7 @@
 def kernel(
     x_hbm, pattern_hbm, count, tiles_hbm, out_ref,
     raw, pattern, padded, table_v, table, tiles, own, held, runs,
-    col, col_scale, row, col_got, scale_got, pieces,
+    col, col_scale, row, leaving, col_got, scale_got, pieces,
     load, tile_sem, x_send, x_recv, col_send, col_recv, scale_send, scale_recv, row_send, row_recv,
 ):
     i, k = lax.axis_index("diag"), lax.axis_index("tri")
@@ -158,7 +173,7 @@
                 pl.when(takers[h][0])(give[h].start)
             pl.when(home)(keep.start)
 
-    visit(False, 0, 0, 192 // UNROLL, acc, table, tiles, own, runs, meet)
+    visit(False, 0, 0, 192 // COL_UNROLL, acc, table, tiles, own, runs, meet)
     lane = lax.broadcasted_iota(jnp.int32, (24, 128), 1)
     scales = jnp.zeros((24, 128), jnp.float32)
     for t in range(8):
@@ -192,7 +207,7 @@
         keep_scale.start()
         keep.wait()
 
-    visit(True, 2, 0, 192 // UNROLL, acc, table, tiles, held, runs)
+    visit(True, 2, 0, 192 // ROW_UNROLL, acc, table, tiles, held, runs)
     @pl.when(home)
     def _():
         keep_col.wait()
@@ -218,16 +233,21 @@
     for n, peer in enumerate([*peers, k]):
         part = [jnp.sum(jnp.where(lane == peer, s, 0.0), axis=1, keepdims=True) for s in scales]
         part = [jnp.broadcast_to(s, (24, 128)) for s in part]
+        totals = []
         for j in range(4):
             p = peer * 4 + j
             total = runs[table[3, p]]
             for slot, scale in zip(slots, part):
                 total = total + col_got[slot, p].astype(jnp.int32).astype(jnp.float32) * scale
-            row[p] = total
+            totals.append(total)
         if n == 7:
+            for j in range(4):
+                row[j] = totals[j]
             break
+        for j, codes in enumerate(packed(totals)):
+            leaving[n, j] = codes
         copy = pltpu.make_async_remote_copy(
-            row.at[pl.ds(peer * 4, 4)],
+            leaving.at[n],
             pieces.at[n],
             row_send.at[n],
             row_recv.at[n],
@@ -251,10 +271,10 @@
 
     for copy in scatter:
         copy.wait()
-    for j in range(4):
-        total = row[k * 4 + j]
-        for n in range(7):
-            total = total + pieces[n, j]
+    totals = [row[j] for j in range(4)]
+    for n in range(7):
+        totals = [a + b for a, b in zip(totals, unpacked(pieces.at[n]))]
+    for j, total in enumerate(totals):
         for p in range(12):
             out_ref[p, :, j * 128 : (j + 1) * 128] = total[2 * p : 2 * p + 2, :]
 
@@ -268,14 +288,15 @@
     f32, bf16, i32 = jnp.float32, jnp.bfloat16, jnp.int32
     dma = pltpu.SemaphoreType.DMA
     block = (columns, size)
+    hbm = functools.partial(pltpu.with_memory_space_constraint, memory_space=pltpu.HBM)
     out = pl.pallas_call(
         kernel,
         out_shape=jax.ShapeDtypeStruct((vecs, sets, rows // tri), f32),
         in_specs=[
-            pl.BlockSpec(memory_space=pl.ANY),
-            pl.BlockSpec(memory_space=pl.ANY),
+            pl.BlockSpec(memory_space=pltpu.HBM),
+            pl.BlockSpec(memory_space=pltpu.HBM),
             pl.BlockSpec(memory_space=pltpu.SMEM),
-            pl.BlockSpec(memory_space=pl.ANY),
+            pl.BlockSpec(memory_space=pltpu.HBM),
         ],
         out_specs=pl.BlockSpec(memory_space=pltpu.VMEM),
         scratch_shapes=[
@@ -290,10 +311,11 @@
             pltpu.VMEM((slots + 8, *block), f32),
             pltpu.VMEM((blocks, *block), jnp.int16),
             pltpu.VMEM(block, f32),
-            pltpu.VMEM((blocks, *block), f32),
+            pltpu.VMEM((4, *block), f32),
+            pltpu.VMEM((7, 5, *block), jnp.int16),
             pltpu.VMEM((3, blocks, *block), jnp.int16),
             pltpu.VMEM((3, *block), f32),
-            pltpu.VMEM((7, 4, *block), f32),
+            pltpu.VMEM((7, 5, *block), jnp.int16),
             dma((3,)),
             dma((CHUNKS,)),
             dma((2,)),
@@ -306,10 +328,10 @@
             dma((7,)),
         ],
         compiler_params=pltpu.CompilerParams(
-            collective_id=0, has_side_effects=True, vmem_limit_bytes=63 << 20
+            collective_id=0, has_side_effects=True, vmem_limit_bytes=40 << 20
         ),
         name="block_products",
-    )(trial_sets.transpose(1, 0, 2), tile_pattern[0, 0], tile_count, tile_values[0, 0])
+    )(hbm(trial_sets.transpose(1, 0, 2)), hbm(tile_pattern[0, 0]), tile_count, hbm(tile_values[0, 0]))
     return out.transpose(1, 0, 2)
 
 

time: 34.2 us -> 31.4 us (0.918)
  the two profiles are of different devices: /device:TPU:24 before, /device:TPU:6 now
where the time goes in v5:
time: 31.4 us; the launch traced here: 31.3 us
  Pallas kernels  30 us (96%)
  between operations  0.66 us (2%)
  local copies, waits for them, and re-layouts  0.62 us (2%)
    pallas_call x1, Pallas kernels, local(): pl.pallas_call(kernel, out_shape=jax.ShapeDtypeStruct((vecs, sets, rows /...  30 us

profile of v5, /device:TPU:6, one launch (start us, length us, event | category | flops | bytes accessed | tf_op | source)
XLA Modules:
  0.0 31.3 jit_solution(18186589757408062007)
XLA Ops:
  0.7 30.0 %block_products.1 = f32[12,2,512]{2,1,0:T(2,128)S(1)} custom-call(bf16[12,2,4096]{2,1,0:T(2,128)(2,1)} %bitcast.6, s32[2,192]{1,0:T(2,128)} %bitcast.7, s32[1,1]{1,0:T(1,128)S(6)} %copy.6.count, bf16[192,128,128]{2,1,0:T(8,128)(2,1)} %bitcast.5), custom_call_target="tpu_custom_call" | custom-call | tf_op jit(solution)/shard_map/block_products/pallas_call | solution.py:292
  30.7 0.6 %copy.7 = f32[2,12,512]{2,0,1:T(2,128)} copy(f32[2,12,512]{2,0,1:T(2,128)S(1)} %bitcast.4) | data formatting | bytes 98304

commit v6 on v5

--- a/solution.py
+++ b/solution.py
@@ -9,6 +9,7 @@
 
 MESH = pl.DeviceIdType.MESH
 COL_UNROLL = 32
+MEETINGS = 0o10000123
 ROW_UNROLL = 48
 CHUNKS = 8
 
@@ -137,6 +138,24 @@
     whole = jnp.concatenate([raw[p] for p in range(12)], 0)
     for c in range(32):
         own[c] = whole[:, c * 128 : (c + 1) * 128]
+    meeting = ((MEETINGS >> (3 * (((i >> 1) & 3) + 4 * z_hi))) & 7) - 1
+    give = []
+    for h in (0, 1):
+        takes, user = takers[h]
+        give.append(
+            pltpu.make_async_remote_copy(own, held, x_send.at[h], x_recv, device_id=user, device_id_type=MESH)
+        )
+    keep = pltpu.make_async_copy(own, held, x_recv)
+
+    def meet(step):
+        @pl.when(step == meeting)
+        def _():
+            pl.semaphore_wait(barrier, expected)
+            for h in (0, 1):
+                pl.when(takers[h][0])(give[h].start)
+            pl.when(home)(keep.start)
+
+    meet(-1)
     get_pattern.wait()
     padded[:, 0:192] = pattern[...]
     padded[:, 192:256] = jnp.zeros((2, 64), jnp.int32)
@@ -156,23 +175,6 @@
     for copy in get_tiles:
         copy.wait()
     acc = jnp.zeros((24, 128), jnp.float32)
-    meeting = jnp.where(z_hi == 0, jnp.maximum(2 - ((i >> 1) & 3), 0), 0)
-    give = []
-    for h in (0, 1):
-        takes, user = takers[h]
-        give.append(
-            pltpu.make_async_remote_copy(own, held, x_send.at[h], x_recv, device_id=user, device_id_type=MESH)
-        )
-    keep = pltpu.make_async_copy(own, held, x_recv)
-
-    def meet(step):
-        @pl.when(step == meeting)
-        def _():
-            pl.semaphore_wait(barrier, expected)
-            for h in (0, 1):
-                pl.when(takers[h][0])(give[h].start)
-            pl.when(home)(keep.start)
-
     visit(False, 0, 0, 192 // COL_UNROLL, acc, table, tiles, own, runs, meet)
     lane = lax.broadcasted_iota(jnp.int32, (24, 128), 1)
     scales = jnp.zeros((24, 128), jnp.float32)
@@ -257,6 +259,13 @@
         copy.start()
         scatter.append(copy)
 
+    totals = [row[j] for j in range(4)]
+    for n in (4, 5, 6, 3, 0, 1, 2):
+        scatter[n].wait_recv()
+        totals = [a + b for a, b in zip(totals, unpacked(pieces.at[n]))]
+    for j, total in enumerate(totals):
+        for p in range(12):
+            out_ref[p, :, j * 128 : (j + 1) * 128] = total[2 * p : 2 * p + 2, :]
     for h in (0, 1):
         takes, user = takers[h]
 
@@ -268,15 +277,8 @@
     def _():
         for copy in back:
             copy.wait_send()
-
     for copy in scatter:
-        copy.wait()
-    totals = [row[j] for j in range(4)]
-    for n in range(7):
-        totals = [a + b for a, b in zip(totals, unpacked(pieces.at[n]))]
-    for j, total in enumerate(totals):
-        for p in range(12):
-            out_ref[p, :, j * 128 : (j + 1) * 128] = total[2 * p : 2 * p + 2, :]
+        copy.wait_send()
 
 
 def local(trial_sets, tile_values, tile_pattern, tile_count):

time: 31.4 us -> 30.5 us (0.971)
  the two profiles are of different devices: /device:TPU:6 before, /device:TPU:1 now
where the time goes in v6:
time: 30.5 us; the launch traced here: 30.4 us
  Pallas kernels  29.1 us (95%)
  between operations  0.66 us (2%)
  local copies, waits for them, and re-layouts  0.62 us (2%)
    pallas_call x1, Pallas kernels, local(): pl.pallas_call(kernel, out_shape=jax.ShapeDtypeStruct((vecs, sets, rows /...  29.1 us
    unnamed x1, local copies, waits for them, and re-layouts  0.62 us

profile of v6, /device:TPU:1, one launch (start us, length us, event | category | flops | bytes accessed | tf_op | source)
XLA Modules:
  0.0 30.4 jit_solution(3961300855419565228)
XLA Ops:
  0.7 29.1 %block_products.1 = f32[12,2,512]{2,1,0:T(2,128)S(1)} custom-call(bf16[12,2,4096]{2,1,0:T(2,128)(2,1)} %bitcast.6, s32[2,192]{1,0:T(2,128)} %bitcast.7, s32[1,1]{1,0:T(1,128)S(6)} %copy.6.count, bf16[192,128,128]{2,1,0:T(8,128)(2,1)} %bitcast.5), custom_call_target="tpu_custom_call" | custom-call | tf_op jit(solution)/shard_map/block_products/pallas_call | solution.py:294
  29.8 0.6 %copy.7 = f32[2,12,512]{2,0,1:T(2,128)} copy(f32[2,12,512]{2,0,1:T(2,128)S(1)} %bitcast.4) | data formatting | bytes 98304

commit v7 on v6

--- a/solution.py
+++ b/solution.py
@@ -110,7 +110,7 @@
         user = (i + 4 * h + x) & 31
         takes = (half_of(user, h, x) == z_hi) & jnp.logical_not((h * 4 + x) == 0)
         takers.append((takes, {"diag": user, "tri": h * 4 + x}))
-    peers = [((1 - z_hi) * 4 + ((x + d) & 3)) for d in (2, 1, 3, 0)] + [z_hi * 4 + ((x + d) & 3) for d in (2, 1, 3)]
+    peers = [((1 - z_hi) * 4 + ((x + d) & 3)) for d in (2, 3, 1, 0)] + [z_hi * 4 + ((x + d) & 3) for d in (2, 3, 1)]
 
     get_pattern = pltpu.make_async_copy(pattern_hbm, pattern, load.at[0])
     get_x = pltpu.make_async_copy(x_hbm, raw, load.at[1])

time: 30.5 us -> 30.2 us (level)
    pallas_call x1, Pallas kernels: 29.1 us -> 28.8 us  [local(): pl.pallas_call(kernel, out_shape=jax.ShapeDtypeStruct((vecs, sets, rows /...]
where the time goes in v7:
time: 30.2 us; the launch traced here: 30.1 us
  Pallas kernels  28.8 us (95%)
  between operations  0.66 us (2%)
  local copies, waits for them, and re-layouts  0.62 us (2%)
    pallas_call x1, Pallas kernels, local(): pl.pallas_call(kernel, out_shape=jax.ShapeDtypeStruct((vecs, sets, rows /...  28.8 us
    unnamed x1, local copies, waits for them, and re-layouts  0.62 us

profile of v7, /device:TPU:1, one launch (start us, length us, event | category | flops | bytes accessed | tf_op | source)
XLA Modules:
  0.0 30.1 jit_solution(12122556730491183377)
XLA Ops:
  0.7 28.8 %block_products.1 = f32[12,2,512]{2,1,0:T(2,128)S(1)} custom-call(bf16[12,2,4096]{2,1,0:T(2,128)(2,1)} %bitcast.6, s32[2,192]{1,0:T(2,128)} %bitcast.7, s32[1,1]{1,0:T(1,128)S(6)} %copy.6.count, bf16[192,128,128]{2,1,0:T(8,128)(2,1)} %bitcast.5), custom_call_target="tpu_custom_call" | custom-call | tf_op jit(solution)/shard_map/block_products/pallas_call | solution.py:294
  29.5 0.6 %copy.7 = f32[2,12,512]{2,0,1:T(2,128)} copy(f32[2,12,512]{2,0,1:T(2,128)S(1)} %bitcast.4) | data formatting | bytes 98304

commit v8 on v7

--- a/solution.py
+++ b/solution.py
@@ -110,7 +110,8 @@
         user = (i + 4 * h + x) & 31
         takes = (half_of(user, h, x) == z_hi) & jnp.logical_not((h * 4 + x) == 0)
         takers.append((takes, {"diag": user, "tri": h * 4 + x}))
-    peers = [((1 - z_hi) * 4 + ((x + d) & 3)) for d in (2, 3, 1, 0)] + [z_hi * 4 + ((x + d) & 3) for d in (2, 3, 1)]
+    turn = 1 - 2 * (i & 1)
+    peers = [((1 - z_hi) * 4 + ((x + turn * d) & 3)) for d in (2, 1, 3, 0)] + [z_hi * 4 + ((x + turn * d) & 3) for d in (2, 1, 3)]
 
     get_pattern = pltpu.make_async_copy(pattern_hbm, pattern, load.at[0])
     get_x = pltpu.make_async_copy(x_hbm, raw, load.at[1])

time: 30.2 us -> 30.2 us (level)
  no operation moved by 1% of the time
where the time goes in v8:
time: 30.2 us; the launch traced here: 30.1 us
  Pallas kernels  28.8 us (95%)
  between operations  0.66 us (2%)
  local copies, waits for them, and re-layouts  0.62 us (2%)
    pallas_call x1, Pallas kernels, local(): pl.pallas_call(kernel, out_shape=jax.ShapeDtypeStruct((vecs, sets, rows /...  28.8 us
    unnamed x1, local copies, waits for them, and re-layouts  0.62 us

profile of v8, /device:TPU:1, one launch (start us, length us, event | category | flops | bytes accessed | tf_op | source)
XLA Modules:
  0.0 30.1 jit_solution(10729928307563947377)
XLA Ops:
  0.7 28.8 %block_products.1 = f32[12,2,512]{2,1,0:T(2,128)S(1)} custom-call(bf16[12,2,4096]{2,1,0:T(2,128)(2,1)} %bitcast.6, s32[2,192]{1,0:T(2,128)} %bitcast.7, s32[1,1]{1,0:T(1,128)S(6)} %copy.6.count, bf16[192,128,128]{2,1,0:T(8,128)(2,1)} %bitcast.5), custom_call_target="tpu_custom_call" | custom-call | tf_op jit(solution)/shard_map/block_products/pallas_call | solution.py:295
  29.5 0.6 %copy.7 = f32[2,12,512]{2,0,1:T(2,128)} copy(f32[2,12,512]{2,0,1:T(2,128)S(1)} %bitcast.4) | data formatting | bytes 98304
